TPU v7x, 32 devices: a whole 2x2x4 slice. The times are simulated.
32 devices in a mesh: seq: 8 (over y, x, core), head: 4 (over z).
Axes of the slice: x: 2, y: 2, z: 4, core: 2. Of those that a mesh axis runs over, the one named last changes fastest.
Arguments:
- prefix_k: bfloat16 [8, 4096, 1024], P('seq', None, 'head'), may hold values from -7 to 7
- prefix_v: bfloat16 [8, 4096, 1024], P('seq', None, 'head'), may hold values from -6 to 6
- queries: bfloat16 [4096, 4096], P('seq', 'head'), may hold values from -100 to 100
- suffix_k: bfloat16 [4096, 1024], P('seq', 'head'), may hold values from -6 to 6
- suffix_v: bfloat16 [4096, 1024], P('seq', 'head'), may hold values from -6 to 6
- residual: bfloat16 [4096, 8192], P('seq', 'head'), may hold values from -12 to 12
- out_weight: bfloat16 [8192, 4096], P('seq', 'head'), may hold values from -2 to 2
- norm_gain: float32 [8192], replicated, may hold values from 0.25 to 1.75
- value_weight: float32 [8192], replicated, may hold values from -0.0029296875 to 0.0029296875
- prompt_of: int32 [8], replicated, may hold values from 0 to 7
- suffix_len: int32 [8], replicated, may hold values from 128 to 512
- return_table: float32 [512], replicated, may hold values from -4 to 4
- return_index: int32 [4096], P('seq'), may hold values from 0 to 511
Outputs:
- cache_k: bfloat16 [8, 4096, 1024], P(None, 'seq', 'head')
- cache_v: bfloat16 [8, 4096, 1024], P(None, 'seq', 'head')
- hidden: bfloat16 [4096, 8192], P('seq', 'head')
- values: float32 [4096], P('seq')
- grad_out: float32 [8192, 4096], P('seq', 'head')
All inputs are finite; a program needn't handle non-finite values.
Results may differ from a plain program's by a relative error of at most 0.014.
Values may be sent and summed in bfloat16 or wider, within the bound.
No kernel may reach another device: no remote copies, remote signals or barrier semaphores. Data moves between devices by JAX's collectives and lax.ppermute only.
A program may use at most 192 MiB of HBM per device.

v0:
```python
import jax
import jax.numpy as jnp
from jax import lax
from jax.sharding import PartitionSpec as P

D = 8192
KVH = 8
HD = 128
HQ = 32
BINS = 512
EPSILON = 1e-05
MASKED = -1e30


def attention(query_rows, prompt_keys, prompt_values, own_keys, own_values):
    row_count = query_rows.shape[0]
    kv_heads = prompt_keys.shape[1] // HD
    group_size = HQ // KVH
    prefix_count = prompt_keys.shape[0]
    key_rows = jnp.concatenate([prompt_keys, own_keys], 0)
    span_len = key_rows.shape[0]
    key_rows = key_rows.reshape(span_len, kv_heads, HD)
    value_rows = jnp.concatenate([prompt_values, own_values], 0).reshape(span_len, kv_heads, HD)
    query_block = query_rows.reshape(row_count, kv_heads, group_size, HD)
    scores = jnp.einsum(
        "skgd,lkd->kgsl", query_block, key_rows, preferred_element_type=jnp.float32
    ) * HD ** (-0.5)
    key_pos = jnp.arange(span_len)[None, :]
    query_pos = jnp.arange(row_count)[:, None]
    allowed = (key_pos < prefix_count) | (key_pos - prefix_count <= query_pos)
    scores = jnp.where(allowed, scores, MASKED)
    row_max = jnp.max(scores, -1, keepdims=True)
    weights = jnp.exp(scores - row_max)
    totals = jnp.sum(weights, -1, keepdims=True)
    mixed = jnp.einsum(
        "kgsl,lkd->skgd",
        weights.astype(jnp.bfloat16),
        value_rows,
        preferred_element_type=jnp.float32,
    )
    mixed = mixed / jnp.transpose(totals, (2, 0, 1, 3))
    return mixed.reshape(row_count, kv_heads * group_size * HD).astype(jnp.bfloat16)


def local(
    prefix_k,
    prefix_v,
    queries,
    suffix_k,
    suffix_v,
    residual,
    out_weight,
    norm_gain,
    value_weight,
    prompt_of,
    suffix_len,
    return_table,
    return_index,
):
    cache_k, cache_v = (
        lax.all_to_all(prefix_k, "seq", split_axis=1, concat_axis=0, tiled=True),
        lax.all_to_all(prefix_v, "seq", split_axis=1, concat_axis=0, tiled=True),
    )
    chosen_k = jnp.take(cache_k, prompt_of, axis=0)
    chosen_v = jnp.take(cache_v, prompt_of, axis=0)
    fetched_k, fetched_v = (
        lax.all_to_all(chosen_k, "seq", split_axis=0, concat_axis=1, tiled=True),
        lax.all_to_all(chosen_v, "seq", split_axis=0, concat_axis=1, tiled=True),
    )
    attn = attention(queries, fetched_k[0], fetched_v[0], suffix_k, suffix_v)
    partial_value = lax.dot_general(
        attn,
        lax.all_gather(out_weight, "seq", axis=0, tiled=True),
        (((1,), (1,)), ((), ())),
        preferred_element_type=jnp.float32,
    )
    row_count = residual.shape[0]
    local_width = residual.shape[1]
    head_start = lax.axis_index("head") * local_width
    gain_weight = norm_gain * value_weight
    one_hot = (return_index[:, None] == jnp.arange(BINS)[None, :]).astype(jnp.float32)
    target = jnp.dot(one_hot, return_table, precision=lax.Precision.HIGHEST)
    live = jnp.arange(row_count) < suffix_len[lax.axis_index("seq")]
    totals = lax.psum(partial_value.astype(jnp.bfloat16), "head").astype(jnp.float32)
    residual_full = lax.all_gather(residual, "head", axis=1, tiled=True)
    hidden_full = (residual_full.astype(jnp.float32) + totals).astype(jnp.bfloat16)
    hidden_wide = hidden_full.astype(jnp.float32)
    square_sum = jnp.sum(hidden_wide * hidden_wide, 1)
    weighted_sum = jnp.sum(hidden_wide * gain_weight[None, :], 1)
    inverse = lax.rsqrt(square_sum / D + EPSILON)
    value_rows = weighted_sum * inverse
    error_term = jnp.where(live, value_rows - target, 0.0)
    hidden_grad = (
        error_term[:, None]
        * (
            inverse[:, None] * gain_weight[None, :]
            - (weighted_sum * inverse * inverse * inverse)[:, None] * hidden_wide / D
        )
    ).astype(jnp.bfloat16)
    hidden_out = lax.dynamic_slice_in_dim(hidden_full, head_start, local_width, 1)
    grad_out = lax.psum_scatter(
        lax.dot_general(
            hidden_grad, attn, (((0,), (0,)), ((), ())), preferred_element_type=jnp.float32
        ).astype(jnp.bfloat16),
        "seq",
        scatter_dimension=0,
        tiled=True,
    ).astype(jnp.float32)
    return (cache_k, cache_v, hidden_out, value_rows, grad_out)


def solution(mesh):
    in_specs = (
        P("seq", None, "head"),
        P("seq", None, "head"),
        P("seq", "head"),
        P("seq", "head"),
        P("seq", "head"),
        P("seq", "head"),
        P("seq", "head"),
        P(),
        P(),
        P(),
        P(),
        P(),
        P("seq"),
    )
    out_specs = (
        P(None, "seq", "head"),
        P(None, "seq", "head"),
        P("seq", "head"),
        P("seq"),
        P("seq", "head"),
    )
    return jax.shard_map(local, mesh=mesh, in_specs=in_specs, out_specs=out_specs, check_vma=False)
```

profile of v0, /device:TPU:0, one launch (start us, length us, event | category | flops | bytes accessed | tf_op | source)
XLA Modules:
  0.0 764.6 jit_solution(6455849590809250505)
XLA Ops:
  7.9 7.5 copy.64
  15.9 21.6 %reduce.1 = bf16[4096,256]{1,0:T(8,128)(2,1)S(1)} reduce(bf16[4096,1,256]{2,1,0:T(2,128)(2,1)} %bitcast.55, bf16[]{:T(256)} %broadcast.78), dimensions={1}, to_apply=%bitcast.52.reduce_sub_computation | reduce | bytes 4194306
  40.7 5.3 all-to-all-start.1
  45.9 7.5 copy.65
  53.4 23.1 %reduce = bf16[4096,256]{1,0:T(8,128)(2,1)} reduce(bf16[4096,1,256]{2,1,0:T(2,128)(2,1)} %bitcast.56, bf16[]{:T(256)} %broadcast.78), dimensions={1}, to_apply=%bitcast.53.reduce_sub_computation | reduce | bytes 4194306
  76.4 5.8 reshape.97
  82.3 7.4 all-to-all-done.1
  89.7 4.4 all-to-all-start
  94.1 4.3 reshape.100
  101.0 39.0 %all-to-all-done = bf16[8,2,65536]{2,1,0:T(2,128)(2,1)} async-done(((bf16[8,2,65536]{2,1,0:T(2,128)(2,1)}), bf16[8,2,65536]{2,1,0:T(2,128)(2,1)}, u32[]{:S(2)}, u32[]{:S(2)}) %all-to-all-start) | async-done | bytes 2097184 | tf_op jit(solution)/shard_map/all_to_all | solution.py:61
  140.0 6.7 reshape.98
  160.5 4.5 all-to-all-start.3
  171.7 19.9 %all-to-all-done.3 = bf16[8,512,256]{2,1,0:T(8,128)(2,1)} async-done(((bf16[8,512,256]{2,1,0:T(8,128)(2,1)}), bf16[8,512,256]{2,1,0:T(8,128)(2,1)}, u32[]{:S(2)}, u32[]{:S(2)}) %all-to-all-start.3) | async-done | bytes 2097184 | tf_op jit(solution)/shard_map/all_to_all | solution.py:67
  191.6 4.4 all-to-all-start.2
  203.4 28.3 %fusion.2 = (f32[2,4,512]{2,1,0:T(4,128)S(1)}, f32[2,4608,512,4]{2,1,3,0:T(8,128)}) fusion(pred[512,4608]{0,1:T(8,128)(4,1)S(1)} %fusion.12, bf16[512,2,4,128]{3,2,1,0:T(4,128)(2,1)S(1)} %reshape.68, bf16[512,2,128]{2,0,1:T(8,128)(2,1)} %copy.47, bf16[4096,2,128]{2,0,1:T(8,128)(2,1)} %copy.46), kind=kOutput, calls=%fused_computation.6 | convolution fusion | flops 4893175808 | bytes 81281024 | tf_op jit(solution)/shard_map/skgd,lkd->kgsl/dot_general | solution.py:25
  235.7 6.1 copy.53
  241.8 24.4 %fusion = f32[2,4,512]{2,1,0:T(4,128)S(1)} fusion(f32[2,4608,512,4]{2,1,3,0:T(8,128)} %get-tuple-element.15, f32[2,4,512]{2,1,0:T(4,128)S(1)} %get-tuple-element.14, pred[512,4608]{0,1:T(8,128)(4,1)S(1)} %fusion.12), kind=kLoop, calls=%fused_computation.4 | loop fusion | flops 75493376 | bytes 77889536 | tf_op jit(solution)/shard_map/reduce_sum | solution.py:34
  266.2 29.5 %fusion.24 = bf16[512,2,4,128]{0,3,2,1:T(8,128)(2,1)} fusion(f32[2,4608,512,4]{2,1,3,0:T(8,128)} %get-tuple-element.15, f32[2,4,512]{2,1,0:T(4,128)S(1)} %get-tuple-element.14, pred[512,4608]{0,1:T(8,128)(4,1)S(1)} %fusion.12, bf16[512,2,128]{0,2,1:T(8,128)(2,1)S(1)} %bitcast.64, bf16[4096,2,128]{0,2,1:T(8,128)(2,1)} %copy.53, f32[512,2,4]{0,2,1:T(4,128)S(1)} %bitcast.65), kind=kOutput, calls=%fused_computation.36 | convolution fusion | flops 4913102848 | bytes 81297408 | tf_op jit(solution)/shard_map/kgsl,lkd->skgd/dot_general | solution.py:35
  295.7 14.8 %convolution_convert_fusion.1 = bf16[512,8192]{1,0:T(8,128)(2,1)} fusion(bf16[512,1024]{0,1:T(8,128)(2,1)} %bitcast.67, bf16[8192,1024]{1,0:T(8,128)(2,1)} %all-gather.5.cloned.1.call-done), kind=kOutput, calls=%fused_computation.20 | convolution fusion | flops 8594128896 | bytes 26214400 | tf_op jit(solution)/shard_map/dot_general | solution.py:71
  312.6 6.1 all-gather.3.cloned.1.call-done
  318.7 291.5 %all-reduce.2.cloned.1.call-done = bf16[512,8192]{1,0:T(8,128)(2,1)} async-done(((bf16[512,8192]{1,0:T(8,128)(2,1)}), bf16[512,8192]{1,0:T(8,128)(2,1)}) %all-reduce.2.cloned.1.call-update) | async-done | bytes 8388624 | tf_op jit(solution)/shard_map/psum | solution.py:84
  610.2 10.7 %fusion.7 = (f32[512]{0:T(512)S(1)}, f32[512]{0:T(512)S(1)}, bf16[512,8192]{1,0:T(8,128)(2,1)}) fusion(f32[8192]{0:T(1024)S(1)} %mul.79, bf16[512,8192]{1,0:T(8,128)(2,1)} %all-reduce.2.cloned.1.call-done, bf16[512,8192]{1,0:T(8,128)(2,1)} %all-gather.3.cloned.1.call-done), kind=kLoop, calls=%fused_computation.13 | loop fusion | flops 37747712 | bytes 25202688 | tf_op jit(solution)/shard_map/reduce_sum | solution.py:88
  621.7 17.0 %convolution_convert_fusion = bf16[8192,1024]{1,0:T(8,128)(2,1)} fusion(bf16[512,1024]{0,1:T(8,128)(2,1)S(1)} %bitcast.68, bf16[512,8192]{1,0:T(8,128)(2,1)} %get-tuple-element.10, f32[512]{0:T(512)S(1)} %multiply_multiply_fusion, f32[512]{0:T(512)S(1)} %get-tuple-element.11, f32[512]{0:T(512)S(1)} %get-tuple-element.8, f32[8192]{0:T(1024)S(1)} %mul.79), kind=kOutput, calls=%fused_computation.19 | convolution fusion | flops 8627683328 | bytes 26253312 | tf_op jit(solution)/shard_map/dot_general | solution.py:102
  641.8 112.2 %reduce-scatter.2.cloned.1.call-done = bf16[1024,1024]{1,0:T(8,128)(2,1)} async-done(((bf16[8192,1024]{1,0:T(8,128)(2,1)}), bf16[1024,1024]{1,0:T(8,128)(2,1)}) %reduce-scatter.2.cloned.1.call-update) | async-done | bytes 2097168 | tf_op jit(solution)/shard_map/reduce_scatter | solution.py:101
  (65 shorter events, 48.6 us)
Async XLA Ops:
  7.2 304.7 %copy-start = (f32[512]{0:T(512)S(1)}, f32[512]{0:T(512)}, u32[]{:S(2)}) copy-start(f32[512]{0:T(512)} %param.26) | copy-start | bytes 6148
  7.2 288.5 %all-gather.5.cloned.1.call-start = ((), (), s32[]{:S(2)}) async-start(), calls=%async_computation.6 | async-start | bytes 18874368 | tf_op jit(solution)/shard_map/all_gather | solution.py:73
  40.7 49.0 %all-to-all-start.1 = ((bf16[8,2,65536]{2,1,0:T(2,128)(2,1)}), bf16[8,2,65536]{2,1,0:T(2,128)(2,1)S(1)}, u32[]{:S(2)}, u32[]{:S(2)}) async-start(bf16[8,2,65536]{2,1,0:T(2,128)(2,1)} %reshape.99), calls=%async_computation.1 | async-start | bytes 4194304 | tf_op jit(solution)/shard_map/all_to_all | solution.py:62
  76.4 17.6 %copy-start.11 = (s32[8]{0:T(128)S(1)}, s32[8]{0:T(128)}, u32[]{:S(2)}) copy-start(s32[8]{0:T(128)} %param.24) | copy-start | bytes 100
  89.7 50.3 %all-to-all-start = ((bf16[8,2,65536]{2,1,0:T(2,128)(2,1)}), bf16[8,2,65536]{2,1,0:T(2,128)(2,1)}, u32[]{:S(2)}, u32[]{:S(2)}) async-start(bf16[8,2,65536]{2,1,0:T(2,128)(2,1)} %reshape.97), calls=%async_computation | async-start | bytes 4194304 | tf_op jit(solution)/shard_map/all_to_all | solution.py:61
  101.0 49.6 %copy-start.1 = (bf16[1,4096,256]{2,1,0:T(8,128)(2,1)}, bf16[1,4096,256]{2,1,0:T(8,128)(2,1)S(1)}, u32[]{:S(2)}) copy-start(bf16[1,4096,256]{2,1,0:T(8,128)(2,1)S(1)} %copy.57) | copy-start | bytes 6291460
  152.6 3.7 copy-start.2
  160.5 5.3 copy-start.3
  160.5 6.0 copy-start.4
  160.5 7.0 copy-start.5
  160.5 31.1 %all-to-all-start.3 = ((bf16[8,512,256]{2,1,0:T(8,128)(2,1)}), bf16[8,512,256]{2,1,0:T(8,128)(2,1)}, u32[]{:S(2)}, u32[]{:S(2)}) async-start(bf16[8,512,256]{2,1,0:T(8,128)(2,1)} %get-tuple-element.13), calls=%async_computation.3 | async-start | bytes 4194304 | tf_op jit(solution)/shard_map/all_to_all | solution.py:67
  165.0 153.7 %all-gather.3.cloned.1.call-start = ((), (), s32[]{:S(2)}) async-start(), calls=%async_computation.5 | async-start | bytes 10485760 | tf_op jit(solution)/shard_map/all_gather | solution.py:85
  191.6 40.1 %all-to-all-start.2 = ((bf16[8,512,256]{2,1,0:T(8,128)(2,1)}), bf16[8,512,256]{2,1,0:T(8,128)(2,1)}, u32[]{:S(2)}, u32[]{:S(2)}) async-start(bf16[8,512,256]{2,1,0:T(8,128)(2,1)} %get-tuple-element.12), calls=%async_computation.2 | async-start | bytes 4194304 | tf_op jit(solution)/shard_map/all_to_all | solution.py:68
  196.0 414.2 %all-reduce.2.cloned.1.call-start = ((), (), s32[]{:S(2)}) async-start(), calls=%async_computation.7 | async-start | bytes 16777216 | tf_op jit(solution)/shard_map/psum | solution.py:84
  241.8 24.4 %copy-start.6 = (bf16[512,256]{0,1:T(8,128)(2,1)S(1)}, bf16[512,256]{0,1:T(8,128)(2,1)}, u32[]{:S(2)}) copy-start(bf16[512,256]{0,1:T(8,128)(2,1)} %copy.43) | copy-start | bytes 786436
  310.5 0.8 copy-start.7
  310.5 0.8 copy-start.8
  310.5 0.8 copy-start.12
  310.5 1.4 copy-start.10
  310.6 443.4 %reduce-scatter.2.cloned.1.call-start = ((), (), s32[]{:S(2)}) async-start(), calls=%async_computation.8 | async-start | bytes 18874368 | tf_op jit(solution)/shard_map/reduce_scatter | solution.py:101
  312.5 309.1 %copy-start.13 = (bf16[512,2,4,128]{0,3,2,1:T(8,128)(2,1)S(1)}, bf16[512,2,4,128]{0,3,2,1:T(8,128)(2,1)}, u32[]{:S(2)}) copy-start(bf16[512,2,4,128]{0,3,2,1:T(8,128)(2,1)} %fusion.24) | copy-start | bytes 3145732
  621.6 17.0 %copy-start.9 = (f32[512]{0:T(512)}, f32[512]{0:T(512)S(1)}, u32[]{:S(2)}) copy-start(f32[512]{0:T(512)S(1)} %get-tuple-element.9) | copy-start | bytes 6148
Sparse Core Ops, SparseCore 0:
  9.9 127.5 all-gather.4
  167.4 151.2 all-gather.2
  321.2 289.0 all-reduce.1
  638.8 115.1 reduce-scatter.1
where the time goes:
time: 766 us; the launch traced here: 765 us
  waiting for transfers between devices  478 us (62%)
  other arithmetic  92 us (12%)
  matrix products  90.3 us (12%)
  local copies, waits for them, and re-layouts  72 us (9%)
  starting transfers between devices  18.8 us (2%)
  between operations  14 us (2%)
    psum x1, waiting for transfers between devices, local(): lax.psum(partial_value.astype(jnp.bfloat16), 'head').astype(jnp.float32)  292 us
    reduce_scatter x1, waiting for transfers between devices, local(): lax.psum_scatter(lax.dot_general(hidden_grad, attn, (((0,), (0,)), ((), (...  112 us
    unnamed x2, other arithmetic  44.7 us
    unnamed x39, local copies, waits for them, and re-layouts  43.6 us
    all_to_all x1, waiting for transfers between devices, local(): lax.all_to_all(prefix_k, 'seq', split_axis=1, concat_axis=0, tiled=True)  39 us
    dot_general x1, matrix products, attention(): jnp.einsum('kgsl,lkd->skgd', weights.astype(jnp.bfloat16), value_rows, pr...  29.5 us
    dot_general x1, matrix products, attention(): jnp.einsum('skgd,lkd->kgsl', query_block, key_rows, preferred_element_typ...  28.3 us
    reduce_sum x1, other arithmetic, attention(): totals = jnp.sum(weights, -1, keepdims=True)  24.4 us
  transfers between devices with their start and end apart: 8, of which 6 were waited for; matrix products, arithmetic and copies ran while one was open for 29% of the time, Pallas kernels for 0%

commit v1 on v0

--- a/solution.py
+++ b/solution.py
@@ -81,7 +81,9 @@
     one_hot = (return_index[:, None] == jnp.arange(BINS)[None, :]).astype(jnp.float32)
     target = jnp.dot(one_hot, return_table, precision=lax.Precision.HIGHEST)
     live = jnp.arange(row_count) < suffix_len[lax.axis_index("seq")]
-    totals = lax.psum(partial_value.astype(jnp.bfloat16), "head").astype(jnp.float32)
+    totals = jnp.sum(lax.all_gather(partial_value.astype(jnp.bfloat16), "head"), axis=0).astype(
+        jnp.float32
+    )
     residual_full = lax.all_gather(residual, "head", axis=1, tiled=True)
     hidden_full = (residual_full.astype(jnp.float32) + totals).astype(jnp.bfloat16)
     hidden_wide = hidden_full.astype(jnp.float32)

time: 766 us -> 1190 us (1.55)
  waiting for transfers between devices: 478 us -> 862 us
  blocking collectives: 0 us -> 29.8 us
  other arithmetic: 92 us -> 110 us
    all_gather x0 -> x1, waiting for transfers between devices: none -> 559 us  [local(): lax.all_gather(partial_value.astype(jnp.bfloat16), 'head')]
    psum x1 -> x0, waiting for transfers between devices: 292 us -> none  [local(): lax.psum(partial_value.astype(jnp.bfloat16), 'head').astype(jnp.float32)]
    all_gather x1, waiting for transfers between devices: 6.14 us -> 131 us  [local(): residual_full = lax.all_gather(residual, 'head', axis=1, tiled=True)]
    all_to_all x0 -> x1, blocking collectives: none -> 29.8 us  [local(): lax.all_to_all(chosen_k, 'seq', split_axis=0, concat_axis=1, tiled=True)]
    all_to_all x1 -> x0, waiting for transfers between devices: 19.9 us -> none  [local(): lax.all_to_all(chosen_k, 'seq', split_axis=0, concat_axis=1, tiled=True)]
    reduce_sum x0 -> x1, other arithmetic: none -> 18.7 us  [local(): jnp.sum(lax.all_gather(partial_value.astype(jnp.bfloat16), 'head'), axis=0)]
    all_to_all x1, waiting for transfers between devices: 0.01 us -> 13.3 us  [local(): lax.all_to_all(chosen_v, 'seq', split_axis=0, concat_axis=1, tiled=True)]
  transfers between devices with their start and end apart: 8 -> 7, of which waited for: 6 -> 6; matrix products, arithmetic and copies ran while one was open for 29% -> 19% of each run, Pallas kernels for 0% -> 0%
where the time goes in v1:
time: 1190 us
  waiting for transfers between devices  862 us (72%)
  other arithmetic  110 us (9%)
  matrix products  90.1 us (8%)
  local copies, waits for them, and re-layouts  71.3 us (6%)
  blocking collectives  29.8 us (3%)
  starting transfers between devices  14.4 us (1%)
  between operations  14 us (1%)
    all_gather x1, waiting for transfers between devices, local(): lax.all_gather(partial_value.astype(jnp.bfloat16), 'head')  559 us
    all_gather x1, waiting for transfers between devices, local(): residual_full = lax.all_gather(residual, 'head', axis=1, tiled=True)  131 us
    reduce_scatter x1, waiting for transfers between devices, local(): lax.psum_scatter(lax.dot_general(hidden_grad, attn, (((0,), (0,)), ((), (...  111 us
    unnamed x2, other arithmetic  44.7 us
    unnamed x39, local copies, waits for them, and re-layouts  43 us
    all_to_all x1, waiting for transfers between devices, local(): lax.all_to_all(prefix_k, 'seq', split_axis=1, concat_axis=0, tiled=True)  39 us
    all_to_all x1, blocking collectives, local(): lax.all_to_all(chosen_k, 'seq', split_axis=0, concat_axis=1, tiled=True)  29.8 us
    dot_general x1, matrix products, attention(): jnp.einsum('kgsl,lkd->skgd', weights.astype(jnp.bfloat16), value_rows, pr...  29.4 us
  transfers between devices with their start and end apart: 7, of which 6 were waited for; matrix products, arithmetic and copies ran while one was open for 19% of the time, Pallas kernels for 0%

profile of v1, /device:TPU:0, one launch (start us, length us, event | category | flops | bytes accessed | tf_op | source)
XLA Modules:
  0.0 1191.3 jit_solution(4718409050022164569)
XLA Ops:
  7.9 7.5 copy.64
  15.9 21.6 %reduce.2 = bf16[4096,256]{1,0:T(8,128)(2,1)S(1)} reduce(bf16[4096,1,256]{2,1,0:T(2,128)(2,1)} %bitcast.57, bf16[]{:T(256)} %broadcast.78), dimensions={1}, to_apply=%bitcast.53.reduce_sub_computation | reduce | bytes 4194306
  40.7 5.3 all-to-all-start.1
  45.9 7.5 copy.65
  53.4 23.1 %reduce.1 = bf16[4096,256]{1,0:T(8,128)(2,1)} reduce(bf16[4096,1,256]{2,1,0:T(2,128)(2,1)} %bitcast.58, bf16[]{:T(256)} %broadcast.78), dimensions={1}, to_apply=%bitcast.54.reduce_sub_computation | reduce | bytes 4194306
  76.4 5.8 reshape.98
  82.3 7.4 all-to-all-done.1
  89.7 4.4 all-to-all-start
  101.0 39.0 %all-to-all-done = bf16[8,2,65536]{2,1,0:T(2,128)(2,1)} async-done(((bf16[8,2,65536]{2,1,0:T(2,128)(2,1)}), bf16[8,2,65536]{2,1,0:T(2,128)(2,1)}, u32[]{:S(2)}, u32[]{:S(2)}) %all-to-all-start) | async-done | bytes 2097184 | tf_op jit(solution)/shard_map/all_to_all | solution.py:61
  140.0 6.7 reshape.99
  159.8 29.8 %all_to_all.42 = bf16[8,512,256]{2,1,0:T(8,128)(2,1)} all-to-all(bf16[8,512,256]{2,1,0:T(8,128)(2,1)S(1)} %get-tuple-element.13), channel_id=1, replica_groups=mesh['seq'=8,'head'=4] {'seq'}, dimensions={0} | all-to-all | bytes 4194304 | tf_op jit(solution)/shard_map/all_to_all | solution.py:67
  189.7 4.5 all-to-all-start.2
  207.5 13.3 %all-to-all-done.2 = bf16[8,512,256]{2,1,0:T(8,128)(2,1)} async-done(((bf16[8,512,256]{2,1,0:T(8,128)(2,1)}), bf16[8,512,256]{2,1,0:T(8,128)(2,1)}, u32[]{:S(2)}, u32[]{:S(2)}) %all-to-all-start.2) | async-done | bytes 2097184 | tf_op jit(solution)/shard_map/all_to_all | solution.py:68
  224.7 6.1 copy.53
  230.9 28.2 %fusion.2 = (f32[2,4,512]{2,1,0:T(4,128)S(1)}, f32[2,4608,512,4]{2,1,3,0:T(8,128)}) fusion(pred[512,4608]{0,1:T(8,128)(4,1)S(1)} %fusion.12, bf16[512,2,4,128]{3,2,1,0:T(4,128)(2,1)S(1)} %reshape.68, bf16[512,2,128]{2,0,1:T(8,128)(2,1)} %copy.47, bf16[4096,2,128]{2,0,1:T(8,128)(2,1)} %copy.46), kind=kOutput, calls=%fused_computation.6 | convolution fusion | flops 4893175808 | bytes 81281024 | tf_op jit(solution)/shard_map/skgd,lkd->kgsl/dot_general | solution.py:25
  259.1 24.0 %fusion = f32[2,4,512]{2,1,0:T(4,128)S(1)} fusion(f32[2,4608,512,4]{2,1,3,0:T(8,128)} %get-tuple-element.15, f32[2,4,512]{2,1,0:T(4,128)S(1)} %get-tuple-element.14, pred[512,4608]{0,1:T(8,128)(4,1)S(1)} %fusion.12), kind=kLoop, calls=%fused_computation.4 | loop fusion | flops 75493376 | bytes 77889536 | tf_op jit(solution)/shard_map/reduce_sum | solution.py:34
  283.2 29.4 %fusion.24 = bf16[512,2,4,128]{0,3,2,1:T(8,128)(2,1)} fusion(f32[2,4608,512,4]{2,1,3,0:T(8,128)} %get-tuple-element.15, f32[2,4,512]{2,1,0:T(4,128)S(1)} %get-tuple-element.14, pred[512,4608]{0,1:T(8,128)(4,1)S(1)} %fusion.12, bf16[512,2,128]{0,2,1:T(8,128)(2,1)S(1)} %bitcast.66, bf16[4096,2,128]{0,2,1:T(8,128)(2,1)} %copy.53, f32[512,2,4]{0,2,1:T(4,128)S(1)} %bitcast.67), kind=kOutput, calls=%fused_computation.36 | convolution fusion | flops 4913102848 | bytes 81297408 | tf_op jit(solution)/shard_map/kgsl,lkd->skgd/dot_general | solution.py:35
  312.6 14.8 %convolution_convert_fusion.1 = bf16[512,8192]{1,0:T(8,128)(2,1)} fusion(bf16[512,1024]{0,1:T(8,128)(2,1)} %bitcast.69, bf16[8192,1024]{1,0:T(8,128)(2,1)} %all-gather.7.cloned.1.call-done), kind=kOutput, calls=%fused_computation.20 | convolution fusion | flops 8594128896 | bytes 26214400 | tf_op jit(solution)/shard_map/dot_general | solution.py:71
  329.5 558.9 %all-gather.9.cloned.1.call-done = bf16[2048,8192]{1,0:T(8,128)(2,1)} async-done(((bf16[512,8192]{1,0:T(8,128)(2,1)}), bf16[2048,8192]{1,0:T(8,128)(2,1)}) %all-gather.9.cloned.1.call-update) | async-done | bytes 33554448 | tf_op jit(solution)/shard_map/all_gather | solution.py:84
  888.4 18.7 %reduce_sum.40 = bf16[512,8192]{1,0:T(8,128)(2,1)} reduce(bf16[4,512,8192]{2,1,0:T(8,128)(2,1)} %bitcast.56, bf16[]{:T(256)} %constant.17.clone.1), dimensions={0}, to_apply=%region_2.4 | reduce | flops 12582912 | bytes 41943040 | tf_op jit(solution)/shard_map/reduce_sum | solution.py:84
  907.1 130.7 %all-gather.5.cloned.1.call-done = bf16[512,8192]{1,0:T(8,128)(2,1)} async-done(((bf16[512,2048]{1,0:T(8,128)(2,1)}), bf16[512,8192]{1,0:T(8,128)(2,1)}) %all-gather.5.cloned.1.call-update) | async-done | bytes 8388624 | tf_op jit(solution)/shard_map/all_gather | solution.py:87
  1037.8 10.7 fusion.7
  1049.2 17.0 %convolution_convert_fusion = bf16[8192,1024]{1,0:T(8,128)(2,1)} fusion(bf16[512,1024]{0,1:T(8,128)(2,1)S(1)} %bitcast.70, bf16[512,8192]{1,0:T(8,128)(2,1)} %get-tuple-element.10, f32[512]{0:T(512)S(1)} %multiply_multiply_fusion, f32[512]{0:T(512)S(1)} %get-tuple-element.11, f32[512]{0:T(512)S(1)} %get-tuple-element.8, f32[8192]{0:T(1024)S(1)} %mul.79), kind=kOutput, calls=%fused_computation.19 | convolution fusion | flops 8627683328 | bytes 26253312 | tf_op jit(solution)/shard_map/dot_general | solution.py:104
  1069.4 111.4 %reduce-scatter.2.cloned.1.call-done = bf16[1024,1024]{1,0:T(8,128)(2,1)} async-done(((bf16[8192,1024]{1,0:T(8,128)(2,1)}), bf16[1024,1024]{1,0:T(8,128)(2,1)}) %reduce-scatter.2.cloned.1.call-update) | async-done | bytes 2097168 | tf_op jit(solution)/shard_map/reduce_scatter | solution.py:103
  (65 shorter events, 51.6 us)
Async XLA Ops:
  7.2 321.7 %copy-start = (f32[512]{0:T(512)S(1)}, f32[512]{0:T(512)}, u32[]{:S(2)}) copy-start(f32[512]{0:T(512)} %param.26) | copy-start | bytes 6148
  7.2 305.4 %all-gather.7.cloned.1.call-start = ((), (), s32[]{:S(2)}) async-start(), calls=%async_computation.6 | async-start | bytes 18874368 | tf_op jit(solution)/shard_map/all_gather | solution.py:73
  40.7 49.0 %all-to-all-start.1 = ((bf16[8,2,65536]{2,1,0:T(2,128)(2,1)}), bf16[8,2,65536]{2,1,0:T(2,128)(2,1)S(1)}, u32[]{:S(2)}, u32[]{:S(2)}) async-start(bf16[8,2,65536]{2,1,0:T(2,128)(2,1)} %reshape.100), calls=%async_computation.1 | async-start | bytes 4194304 | tf_op jit(solution)/shard_map/all_to_all | solution.py:62
  76.4 17.6 %copy-start.11 = (s32[8]{0:T(128)S(1)}, s32[8]{0:T(128)}, u32[]{:S(2)}) copy-start(s32[8]{0:T(128)} %param.24) | copy-start | bytes 100
  89.7 50.3 %all-to-all-start = ((bf16[8,2,65536]{2,1,0:T(2,128)(2,1)}), bf16[8,2,65536]{2,1,0:T(2,128)(2,1)}, u32[]{:S(2)}, u32[]{:S(2)}) async-start(bf16[8,2,65536]{2,1,0:T(2,128)(2,1)} %reshape.98), calls=%async_computation | async-start | bytes 4194304 | tf_op jit(solution)/shard_map/all_to_all | solution.py:61
  101.0 49.6 %copy-start.1 = (bf16[1,4096,256]{2,1,0:T(8,128)(2,1)}, bf16[1,4096,256]{2,1,0:T(8,128)(2,1)S(1)}, u32[]{:S(2)}) copy-start(bf16[1,4096,256]{2,1,0:T(8,128)(2,1)S(1)} %copy.57) | copy-start | bytes 6291460
  152.6 3.7 copy-start.2
  159.8 34.6 %copy-start.3 = (bf16[512,1024]{1,0:T(8,128)(2,1)S(1)}, bf16[512,1024]{1,0:T(8,128)(2,1)}, u32[]{:S(2)}) copy-start(bf16[512,1024]{1,0:T(8,128)(2,1)} %param.17) | copy-start | bytes 3145732
  159.8 35.3 %copy-start.4 = (bf16[512,256]{1,0:T(8,128)(2,1)S(1)}, bf16[512,256]{1,0:T(8,128)(2,1)}, u32[]{:S(2)}) copy-start(bf16[512,256]{1,0:T(8,128)(2,1)} %param.18) | copy-start | bytes 786436
  189.7 6.5 copy-start.5
  189.7 31.1 %all-to-all-start.2 = ((bf16[8,512,256]{2,1,0:T(8,128)(2,1)}), bf16[8,512,256]{2,1,0:T(8,128)(2,1)}, u32[]{:S(2)}, u32[]{:S(2)}) async-start(bf16[8,512,256]{2,1,0:T(8,128)(2,1)} %get-tuple-element.12), calls=%async_computation.2 | async-start | bytes 4194304 | tf_op jit(solution)/shard_map/all_to_all | solution.py:68
  194.2 694.2 %all-gather.9.cloned.1.call-start = ((), (), s32[]{:S(2)}) async-start(), calls=%async_computation.8 | async-start | bytes 41943040 | tf_op jit(solution)/shard_map/all_gather | solution.py:84
  259.1 24.1 %copy-start.6 = (bf16[512,256]{0,1:T(8,128)(2,1)S(1)}, bf16[512,256]{0,1:T(8,128)(2,1)}, u32[]{:S(2)}) copy-start(bf16[512,256]{0,1:T(8,128)(2,1)} %copy.43) | copy-start | bytes 786436
  327.4 0.8 copy-start.7
  327.4 0.8 copy-start.8
  327.4 0.9 copy-start.12
  327.4 1.5 copy-start.10
  327.4 710.4 %all-gather.5.cloned.1.call-start = ((), (), s32[]{:S(2)}) async-start(), calls=%async_computation.5 | async-start | bytes 10485760 | tf_op jit(solution)/shard_map/all_gather | solution.py:87
  328.2 852.5 %reduce-scatter.2.cloned.1.call-start = ((), (), s32[]{:S(2)}) async-start(), calls=%async_computation.7 | async-start | bytes 18874368 | tf_op jit(solution)/shard_map/reduce_scatter | solution.py:103
  907.1 142.1 %copy-start.13 = (bf16[512,2,4,128]{0,3,2,1:T(8,128)(2,1)S(1)}, bf16[512,2,4,128]{0,3,2,1:T(8,128)(2,1)}, u32[]{:S(2)}) copy-start(bf16[512,2,4,128]{0,3,2,1:T(8,128)(2,1)} %fusion.24) | copy-start | bytes 3145732
  1049.2 17.0 %copy-start.9 = (f32[512]{0:T(512)}, f32[512]{0:T(512)S(1)}, u32[]{:S(2)}) copy-start(f32[512]{0:T(512)S(1)} %get-tuple-element.9) | copy-start | bytes 6148
Sparse Core Ops, SparseCore 0:
  9.9 127.5 all-gather.6
  327.6 560.7 all-gather.8
  890.0 147.7 all-gather.4
  1066.3 114.3 reduce-scatter.1
